TPU v7x, 32 devices: a whole 2x2x4 slice. The times are simulated.
32 devices in a mesh: fsdp: 8 (over z, x), rep: 4 (over y, core).
Axes of the slice: x: 2, y: 2, z: 4, core: 2. Of those that a mesh axis runs over, the one named last changes fastest.
Arguments:
- video_in: bfloat16 [32, 196, 1024], P(('fsdp', 'rep')), may hold values from -6 to 6
- audio_in: bfloat16 [32, 128, 1024], P(('fsdp', 'rep')), may hold values from -6 to 6
- bottle_in: bfloat16 [32, 8, 1024], P(('fsdp', 'rep')), may hold values from -6 to 6
- video_gain: float32 [1024], replicated, may hold values from 0.5 to 8
- audio_gain: float32 [1024], replicated, may hold values from 0.5 to 8
- video_qkv: bfloat16 [1024, 3072], P('fsdp'), may hold values from -0.18 to 0.18
- video_out: bfloat16 [1024, 1024], P('fsdp'), may hold values from -0.1875 to 0.1875
- audio_qkv: bfloat16 [1024, 3072], P('fsdp'), may hold values from -0.18 to 0.18
- audio_out: bfloat16 [1024, 1024], P('fsdp'), may hold values from -0.1875 to 0.1875
- grad_video: bfloat16 [32, 196, 1024], P(('fsdp', 'rep')), may hold values from -6 to 6
- grad_audio: bfloat16 [32, 128, 1024], P(('fsdp', 'rep')), may hold values from -6 to 6
- grad_bottle: bfloat16 [32, 8, 1024], P(('fsdp', 'rep')), may hold values from -6 to 6
Outputs:
- dvideo_in: bfloat16 [32, 196, 1024], P(('fsdp', 'rep'))
- daudio_in: bfloat16 [32, 128, 1024], P(('fsdp', 'rep'))
- dbottle_in: bfloat16 [32, 8, 1024], P(('fsdp', 'rep'))
- video_qkv_grad: float32 [1024, 3072], P('fsdp')
- video_out_grad: float32 [1024, 1024], P('fsdp')
- audio_qkv_grad: float32 [1024, 3072], P('fsdp')
- audio_out_grad: float32 [1024, 1024], P('fsdp')
- video_gain_grad: float32 [1024], replicated
- audio_gain_grad: float32 [1024], replicated
All inputs are finite; a program needn't handle non-finite values.
Results may differ from a plain program's by a relative error of at most 0.025.
Values may be sent and summed in bfloat16 or wider, within the bound.
A program may use at most 128 MiB of HBM per device.

v0:
```python
import jax
import jax.numpy as jnp
from jax import lax
from jax.sharding import PartitionSpec as P

HEAD = 64


def stream(tokens, bottle, gain, w_qkv, w_out, d_tokens, bottle_half):
    f32 = jnp.float32
    bf16 = jnp.bfloat16
    z_rows = jnp.concatenate([tokens, bottle], 0)
    rows = z_rows.shape[0]
    width = z_rows.shape[1]
    zf = z_rows.astype(f32)
    inverse = lax.rsqrt(jnp.mean(zf * zf, axis=1, keepdims=True) + 1e-06)
    normed = zf * inverse
    hidden = (normed * gain).astype(bf16)
    qkv = jnp.dot(hidden, w_qkv, preferred_element_type=f32).astype(bf16)
    scale = HEAD ** (-0.5)
    query = qkv[:, :width].reshape(rows, -1, HEAD)
    keyed = qkv[:, width : 2 * width].reshape(rows, -1, HEAD)
    valued = qkv[:, 2 * width :].reshape(rows, -1, HEAD)
    scores = jnp.einsum("shd,thd->hst", query, keyed, preferred_element_type=f32) * scale
    probs = jax.nn.softmax(scores, axis=-1)
    pb = probs.astype(bf16)
    att = (
        jnp.einsum("hst,thd->shd", pb, valued, preferred_element_type=f32)
        .reshape(rows, width)
        .astype(bf16)
    )
    d_out = jnp.concatenate([d_tokens.astype(f32), bottle_half], 0)
    dyb = d_out.astype(bf16)
    out_term = jnp.einsum("sd,se->de", att, dyb, preferred_element_type=f32)
    datt = jnp.einsum("se,de->sd", dyb, w_out, preferred_element_type=f32).astype(bf16)
    datt = datt.reshape(rows, -1, HEAD)
    dprob = jnp.einsum("shd,thd->hst", datt, valued, preferred_element_type=f32)
    dvalue = jnp.einsum("hst,shd->thd", pb, datt, preferred_element_type=f32)
    dscore = probs * (dprob - jnp.sum(probs * dprob, axis=-1, keepdims=True)) * scale
    dsb = dscore.astype(bf16)
    dquery = jnp.einsum("hst,thd->shd", dsb, keyed, preferred_element_type=f32)
    dkey = jnp.einsum("hst,shd->thd", dsb, query, preferred_element_type=f32)
    dqkv = jnp.concatenate(
        [dquery.reshape(rows, width), dkey.reshape(rows, width), dvalue.reshape(rows, width)], 1
    ).astype(bf16)
    qkv_term = jnp.einsum("sd,se->de", hidden, dqkv, preferred_element_type=f32)
    dhidden = jnp.einsum("se,de->sd", dqkv, w_qkv, preferred_element_type=f32)
    gain_term = jnp.sum(dhidden * normed, axis=0)
    dnorm = dhidden * gain
    d_z = d_out + inverse * (dnorm - normed * jnp.mean(dnorm * normed, axis=1, keepdims=True))
    return (d_z, qkv_term, out_term, gain_term)


def all_clips(tokens, bottles, gain, w_qkv, w_out, d_tokens, d_bottles):

    def one_clip(carry, item):
        tok, bot, dtok, dbot = item
        half = dbot.astype(jnp.float32) * 0.5
        d_z, qkv_term, out_term, gain_term = stream(tok, bot, gain, w_qkv, w_out, dtok, half)
        return ((carry[0] + qkv_term, carry[1] + out_term, carry[2] + gain_term), d_z)

    width = w_out.shape[0]
    start = (
        jnp.zeros(w_qkv.shape, jnp.float32),
        jnp.zeros(w_out.shape, jnp.float32),
        jnp.zeros((width,), jnp.float32),
    )
    return lax.scan(one_clip, start, (tokens, bottles, d_tokens, d_bottles))


def fetch(qkv_shard, out_shard):
    groups = lax.axis_size("rep")
    place = lax.axis_index("rep")
    qkv_cols = qkv_shard.shape[1] // groups
    out_cols = out_shard.shape[1] // groups
    qkv_part = lax.dynamic_slice_in_dim(qkv_shard, place * qkv_cols, qkv_cols, 1)
    out_part = lax.dynamic_slice_in_dim(out_shard, place * out_cols, out_cols, 1)
    qkv_part, out_part = (
        lax.all_gather(qkv_part, "fsdp", axis=0, tiled=True),
        lax.all_gather(out_part, "fsdp", axis=0, tiled=True),
    )
    return (
        lax.all_gather(qkv_part, "rep", axis=1, tiled=True),
        lax.all_gather(out_part, "rep", axis=1, tiled=True),
    )


def reduce_grads(qkv_term, out_term, count):
    qkv_sum, out_sum = (
        lax.psum_scatter(
            qkv_term.astype(jnp.bfloat16), "rep", scatter_dimension=1, tiled=True
        ).astype(jnp.float32),
        lax.psum_scatter(
            out_term.astype(jnp.bfloat16), "rep", scatter_dimension=1, tiled=True
        ).astype(jnp.float32),
    )
    qkv_sum, out_sum = (
        lax.psum_scatter(
            qkv_sum.astype(jnp.bfloat16), "fsdp", scatter_dimension=0, tiled=True
        ).astype(jnp.float32),
        lax.psum_scatter(
            out_sum.astype(jnp.bfloat16), "fsdp", scatter_dimension=0, tiled=True
        ).astype(jnp.float32),
    )
    qkv_sum, out_sum = (
        lax.all_gather(qkv_sum.astype(jnp.bfloat16), "rep", axis=1, tiled=True).astype(
            qkv_sum.dtype
        ),
        lax.all_gather(out_sum.astype(jnp.bfloat16), "rep", axis=1, tiled=True).astype(
            out_sum.dtype
        ),
    )
    return (qkv_sum / count, out_sum / count)


def per_device(
    video_in,
    audio_in,
    bottle_in,
    video_gain,
    audio_gain,
    video_qkv,
    video_out,
    audio_qkv,
    audio_out,
    grad_video,
    grad_audio,
    grad_bottle,
):
    count = float(video_in.shape[0] * lax.axis_size("fsdp") * lax.axis_size("rep"))
    video_full, video_proj = fetch(video_qkv, video_out)
    video_sums, dz_video = all_clips(
        video_in, bottle_in, video_gain, video_full, video_proj, grad_video, grad_bottle
    )
    audio_full, audio_proj = fetch(audio_qkv, audio_out)
    video_qkv_grad, video_out_grad = reduce_grads(video_sums[0], video_sums[1], count)
    audio_sums, dz_audio = all_clips(
        audio_in, bottle_in, audio_gain, audio_full, audio_proj, grad_audio, grad_bottle
    )
    audio_qkv_grad, audio_out_grad = reduce_grads(audio_sums[0], audio_sums[1], count)
    gain_video, gain_audio = lax.psum((video_sums[2], audio_sums[2]), ("fsdp", "rep"))
    video_len = video_in.shape[1]
    audio_len = audio_in.shape[1]
    dvideo_in = dz_video[:, :video_len].astype(jnp.bfloat16)
    daudio_in = dz_audio[:, :audio_len].astype(jnp.bfloat16)
    dbottle_in = (dz_video[:, video_len:] + dz_audio[:, audio_len:]).astype(jnp.bfloat16)
    return (
        dvideo_in,
        daudio_in,
        dbottle_in,
        video_qkv_grad,
        video_out_grad,
        audio_qkv_grad,
        audio_out_grad,
        gain_video / count,
        gain_audio / count,
    )


def solution(mesh):
    in_specs = (
        P(("fsdp", "rep"), None, None),
        P(("fsdp", "rep"), None, None),
        P(("fsdp", "rep"), None, None),
        P(),
        P(),
        P("fsdp", None),
        P("fsdp", None),
        P("fsdp", None),
        P("fsdp", None),
        P(("fsdp", "rep"), None, None),
        P(("fsdp", "rep"), None, None),
        P(("fsdp", "rep"), None, None),
    )
    out_specs = (
        P(("fsdp", "rep"), None, None),
        P(("fsdp", "rep"), None, None),
        P(("fsdp", "rep"), None, None),
        P("fsdp", None),
        P("fsdp", None),
        P("fsdp", None),
        P("fsdp", None),
        P(),
        P(),
    )
    return jax.shard_map(
        per_device, mesh=mesh, in_specs=in_specs, out_specs=out_specs, check_vma=False
    )
```

profile of v0, /device:TPU:0, one launch (start us, length us, event | category | flops | bytes accessed | tf_op | source)
XLA Modules:
  0.0 717.2 jit_solution(1365999617299398199)
XLA Ops:
  10.8 46.9 %all-gather.7.cloned.1.call-done = bf16[1024,768]{1,0:T(8,128)(2,1)} async-done(((bf16[128,768]{1,0:T(8,128)(2,1)}), bf16[1024,768]{1,0:T(8,128)(2,1)}) %all-gather.7.cloned.1.call-update) | async-done | bytes 1572880 | tf_op jit(solution)/shard_map/all_gather | solution.py:79
  57.8 45.2 %all-gather.13.cloned.1.call-done = bf16[1024,768]{1,0:T(8,128)(2,1)} async-done(((bf16[128,768]{1,0:T(8,128)(2,1)}), bf16[1024,768]{1,0:T(8,128)(2,1)}) %all-gather.13.cloned.1.call-update) | async-done | bytes 1572880 | tf_op jit(solution)/shard_map/all_gather | solution.py:79
  104.0 33.2 %all_gather.38 = bf16[1024,256]{1,0:T(8,128)(2,1)} all-gather(bf16[128,256]{1,0:T(8,128)(2,1)S(1)} %constant_dynamic-slice_fusion.2), channel_id=1, replica_groups=mesh['fsdp'=8,'rep'=4] {'fsdp'}, dimensions={0}, use_global_device_ids=true | all-gather | bytes 589824 | tf_op jit(solution)/shard_map/all_gather | solution.py:80
  138.2 33.3 %all_gather.42 = bf16[1024,256]{1,0:T(8,128)(2,1)} all-gather(bf16[128,256]{1,0:T(8,128)(2,1)S(1)} %constant_dynamic-slice_fusion), channel_id=1, replica_groups=mesh['fsdp'=8,'rep'=4] {'fsdp'}, dimensions={0}, use_global_device_ids=true | all-gather | bytes 589824 | tf_op jit(solution)/shard_map/all_gather | solution.py:80
  184.9 12.2 %all-gather.15.cloned.1.call-done = bf16[1024,3072]{1,0:T(8,128)(2,1)} async-done(((bf16[1024,768]{1,0:T(8,128)(2,1)}), bf16[1024,3072]{1,0:T(8,128)(2,1)}) %all-gather.15.cloned.1.call-update) | async-done | bytes 6291472 | tf_op jit(solution)/shard_map/all_gather | solution.py:83
  210.3 11.1 %all-gather.11.cloned.1.call-done = bf16[1024,1024]{1,0:T(8,128)(2,1)} async-done(((bf16[1024,256]{1,0:T(8,128)(2,1)}), bf16[1024,1024]{1,0:T(8,128)(2,1)}) %all-gather.11.cloned.1.call-update) | async-done | bytes 2097168 | tf_op jit(solution)/shard_map/all_gather | solution.py:84
  226.4 7.7 %fusion.40 = bf16[16,64,204]{2,1,0:T(8,128)(2,1)} fusion(bf16[204,16,64]{0,2,1:T(8,128)(2,1)} %bitcast.95, f32[16,204,204]{1,2,0:T(8,128)} %fusion.113, f32[16,204,204]{1,2,0:T(8,128)} %get-tuple-element.82, f32[16,204]{1,0:T(8,128)S(1)} %get-tuple-element.81), kind=kOutput, calls=%fused_computation.37 | convolution fusion | flops 90102920 | bytes 6175488 | tf_op jit(solution)/shard_map/while/body/eval_jaxpr/hst,shd->thd/dot_general | solution.py:42
  234.2 6.9 fusion.37
  253.8 6.0 fusion.34
  272.9 6.4 reduce-scatter.13.cloned.1.call-done
  279.4 33.6 %reduce-scatter.21.cloned.1.call-done = bf16[1024,256]{1,0:T(8,128)(2,1)} async-done(((bf16[1024,1024]{1,0:T(8,128)(2,1)}), bf16[1024,256]{1,0:T(8,128)(2,1)}) %reduce-scatter.21.cloned.1.call-update) | async-done | bytes 524304 | tf_op jit(solution)/shard_map/reduce_scatter | solution.py:93
  313.1 60.4 %reduce-scatter.9.cloned.1.call-done = bf16[1024,768]{1,0:T(8,128)(2,1)} async-done(((bf16[1024,3072]{1,0:T(8,128)(2,1)}), bf16[1024,768]{1,0:T(8,128)(2,1)}) %reduce-scatter.9.cloned.1.call-update) | async-done | bytes 1572880 | tf_op jit(solution)/shard_map/reduce_scatter | solution.py:90
  373.8 5.5 fusion.56
  380.4 53.4 %reduce-scatter.17.cloned.1.call-done = bf16[1024,768]{1,0:T(8,128)(2,1)} async-done(((bf16[1024,3072]{1,0:T(8,128)(2,1)}), bf16[1024,768]{1,0:T(8,128)(2,1)}) %reduce-scatter.17.cloned.1.call-update) | async-done | bytes 1572880 | tf_op jit(solution)/shard_map/reduce_scatter | solution.py:90
  433.9 5.5 fusion.73
  440.4 39.5 %all-reduce = (f32[1024]{0:T(1024)S(1)}, f32[1024]{0:T(1024)S(1)}) all-reduce(f32[1024]{0:T(1024)S(1)} %get-tuple-element.57, f32[1024]{0:T(1024)S(1)} %get-tuple-element.59), channel_id=1, replica_groups=mesh['fsdp'=8,'rep'=4] {'fsdp','rep'}, use_global_device_ids=true, to_apply=%region_19.20 | all-reduce | flops 2048 | bytes 16384 | tf_op jit(solution)/shard_map/psum | solution.py:141
  481.1 18.8 %reduce-scatter.15.cloned.1.call-done = bf16[128,256]{1,0:T(8,128)(2,1)} async-done(((bf16[1024,256]{1,0:T(8,128)(2,1)}), bf16[128,256]{1,0:T(8,128)(2,1)}) %reduce-scatter.15.cloned.1.call-update) | async-done | bytes 65552 | tf_op jit(solution)/shard_map/reduce_scatter | solution.py:101
  499.9 6.0 all_gather.45
  505.9 58.8 %reduce-scatter.23.cloned.1.call-done = bf16[128,256]{1,0:T(8,128)(2,1)} async-done(((bf16[1024,256]{1,0:T(8,128)(2,1)}), bf16[128,256]{1,0:T(8,128)(2,1)}) %reduce-scatter.23.cloned.1.call-update) | async-done | bytes 65552 | tf_op jit(solution)/shard_map/reduce_scatter | solution.py:101
  564.7 6.0 all_gather.47
  572.4 60.3 %reduce-scatter.11.cloned.1.call-done = bf16[128,768]{1,0:T(8,128)(2,1)} async-done(((bf16[1024,768]{1,0:T(8,128)(2,1)}), bf16[128,768]{1,0:T(8,128)(2,1)}) %reduce-scatter.11.cloned.1.call-update) | async-done | bytes 196624 | tf_op jit(solution)/shard_map/reduce_scatter | solution.py:98
  632.6 8.9 %all_gather.44 = bf16[128,3072]{1,0:T(8,128)(2,1)S(1)} all-gather(bf16[128,768]{1,0:T(8,128)(2,1)} %reduce-scatter.11.cloned.1.call-done), channel_id=1, replica_groups=mesh['fsdp'=8,'rep'=4] {'rep'}, dimensions={1}, use_global_device_ids=true | all-gather | bytes 983040 | tf_op jit(solution)/shard_map/all_gather | solution.py:106
  642.9 57.7 %reduce-scatter.19.cloned.1.call-done = bf16[128,768]{1,0:T(8,128)(2,1)} async-done(((bf16[1024,768]{1,0:T(8,128)(2,1)}), bf16[128,768]{1,0:T(8,128)(2,1)}) %reduce-scatter.19.cloned.1.call-update) | async-done | bytes 196624 | tf_op jit(solution)/shard_map/reduce_scatter | solution.py:98
  700.6 8.8 %all_gather.46 = bf16[128,3072]{1,0:T(8,128)(2,1)S(1)} all-gather(bf16[128,768]{1,0:T(8,128)(2,1)} %reduce-scatter.19.cloned.1.call-done), channel_id=1, replica_groups=mesh['fsdp'=8,'rep'=4] {'rep'}, dimensions={1}, use_global_device_ids=true | all-gather | bytes 983040 | tf_op jit(solution)/shard_map/all_gather | solution.py:106
  (132 shorter events, 70.7 us)
Async XLA Ops:
  7.2 50.5 %all-gather.7.cloned.1.call-start = ((), (), s32[]{:S(2)}) async-start(), calls=%async_computation.8 | async-start | bytes 1769472 | tf_op jit(solution)/shard_map/all_gather | solution.py:79
  9.0 94.0 %all-gather.13.cloned.1.call-start = ((), (), s32[]{:S(2)}) async-start(), calls=%async_computation.11 | async-start | bytes 1769472 | tf_op jit(solution)/shard_map/all_gather | solution.py:79
  10.7 161.2 %all-gather.9.cloned.1.call-start = ((), (), s32[]{:S(2)}) async-start(), calls=%async_computation.9 | async-start | bytes 7864320 | tf_op jit(solution)/shard_map/all_gather | solution.py:83
  57.7 113.9 %copy-start.2 = (bf16[1,196,1024]{2,1,0:T(8,128)(2,1)S(1)}, bf16[1,196,1024]{2,1,0:T(8,128)(2,1)}, u32[]{:S(2)}) copy-start(bf16[1,196,1024]{2,1,0:T(8,128)(2,1)} %param.12) | copy-start | bytes 1204228
  57.7 113.9 %copy-start.13 = (bf16[1,8,1024]{2,1,0:T(8,128)(2,1)S(1)}, bf16[1,8,1024]{2,1,0:T(8,128)(2,1)}, u32[]{:S(2)}) copy-start(bf16[1,8,1024]{2,1,0:T(8,128)(2,1)} %param.14) | copy-start | bytes 49156
  57.7 139.4 %all-gather.15.cloned.1.call-start = ((), (), s32[]{:S(2)}) async-start(), calls=%async_computation.12 | async-start | bytes 7864320 | tf_op jit(solution)/shard_map/all_gather | solution.py:83
  103.0 68.8 %copy-start.15 = (bf16[1,8,1024]{2,1,0:T(8,128)(2,1)S(1)}, bf16[1,8,1024]{2,1,0:T(8,128)(2,1)}, u32[]{:S(2)}) copy-start(bf16[1,8,1024]{2,1,0:T(8,128)(2,1)} %param.23) | copy-start | bytes 49156
  103.0 68.8 %copy-start.12 = (bf16[1,196,1024]{2,1,0:T(8,128)(2,1)S(1)}, bf16[1,196,1024]{2,1,0:T(8,128)(2,1)}, u32[]{:S(2)}) copy-start(bf16[1,196,1024]{2,1,0:T(8,128)(2,1)} %param.21) | copy-start | bytes 1204228
  103.1 68.9 %copy-start.16 = (f32[1024]{0:T(1024)S(1)}, f32[1024]{0:T(1024)}, u32[]{:S(2)}) copy-start(f32[1024]{0:T(1024)} %param.15) | copy-start | bytes 12292
  103.1 118.3 %all-gather.11.cloned.1.call-start = ((), (), s32[]{:S(2)}) async-start(), calls=%async_computation.10 | async-start | bytes 2621440 | tf_op jit(solution)/shard_map/all_gather | solution.py:84
  137.3 112.0 %all-gather.17.cloned.1.call-start = ((), (), s32[]{:S(2)}) async-start(), calls=%async_computation.13 | async-start | bytes 2621440 | tf_op jit(solution)/shard_map/all_gather | solution.py:84
  171.5 107.8 %reduce-scatter.13.cloned.1.call-start = ((), (), s32[]{:S(2)}) async-start(), calls=%async_computation.16 | async-start | bytes 2621440 | tf_op jit(solution)/shard_map/reduce_scatter | solution.py:93
  184.6 12.5 %copy-start.17 = (f32[1024]{0:T(1024)S(1)}, f32[1024]{0:T(1024)}, u32[]{:S(2)}) copy-start(f32[1024]{0:T(1024)} %param.16) | copy-start | bytes 12292
  184.7 128.4 %reduce-scatter.21.cloned.1.call-start = ((), (), s32[]{:S(2)}) async-start(), calls=%async_computation.20 | async-start | bytes 2621440 | tf_op jit(solution)/shard_map/reduce_scatter | solution.py:93
  210.0 163.5 %reduce-scatter.9.cloned.1.call-start = ((), (), s32[]{:S(2)}) async-start(), calls=%async_computation.14 | async-start | bytes 7864320 | tf_op jit(solution)/shard_map/reduce_scatter | solution.py:90
  226.4 7.7 %copy-start.8 = (bf16[204,1024]{0,1:T(8,128)(2,1)S(1)}, bf16[204,1024]{0,1:T(8,128)(2,1)}, u32[]{:S(2)}) copy-start(bf16[204,1024]{0,1:T(8,128)(2,1)} %copy-done.7) | copy-start | bytes 1253380
  249.2 184.7 %reduce-scatter.17.cloned.1.call-start = ((), (), s32[]{:S(2)}) async-start(), calls=%async_computation.18 | async-start | bytes 7864320 | tf_op jit(solution)/shard_map/reduce_scatter | solution.py:90
  272.9 101.0 %copy-start.19 = (bf16[16,64,204]{2,1,0:T(8,128)(2,1)S(1)}, bf16[16,64,204]{2,1,0:T(8,128)(2,1)}, u32[]{:S(2)}) copy-start(bf16[16,64,204]{2,1,0:T(8,128)(2,1)} %fusion.40) | copy-start | bytes 1253380
  272.9 227.0 %reduce-scatter.15.cloned.1.call-start = ((), (), s32[]{:S(2)}) async-start(), calls=%async_computation.17 | async-start | bytes 589824 | tf_op jit(solution)/shard_map/reduce_scatter | solution.py:101
  279.4 285.3 %reduce-scatter.23.cloned.1.call-start = ((), (), s32[]{:S(2)}) async-start(), calls=%async_computation.21 | async-start | bytes 589824 | tf_op jit(solution)/shard_map/reduce_scatter | solution.py:101
  313.1 319.5 %reduce-scatter.11.cloned.1.call-start = ((), (), s32[]{:S(2)}) async-start(), calls=%async_computation.15 | async-start | bytes 1769472 | tf_op jit(solution)/shard_map/reduce_scatter | solution.py:98
  373.6 327.0 %reduce-scatter.19.cloned.1.call-start = ((), (), s32[]{:S(2)}) async-start(), calls=%async_computation.19 | async-start | bytes 1769472 | tf_op jit(solution)/shard_map/reduce_scatter | solution.py:98
  379.6 54.3 %copy-start.22 = (bf16[16,64,136]{2,1,0:T(8,128)(2,1)S(1)}, bf16[16,64,136]{2,1,0:T(8,128)(2,1)}, u32[]{:S(2)}) copy-start(bf16[16,64,136]{2,1,0:T(8,128)(2,1)} %fusion.34) | copy-start | bytes 835588
  641.5 69.1 %copy-start.1 = (bf16[128,3072]{1,0:T(8,128)(2,1)S(1)}, bf16[128,3072]{1,0:T(8,128)(2,1)}, u32[]{:S(2)}) copy-start(bf16[128,3072]{1,0:T(8,128)(2,1)} %param.17) | copy-start | bytes 2359300
  (16 other events, 45.3 us)
Sparse Core Ops, SparseCore 0:
  10.8 46.8 all-gather.6
  60.4 42.5 all-gather.12
  104.6 44.7 all-gather.8
  150.8 46.3 all-gather.14
  198.6 22.8 all-gather.10
  222.8 22.8 all-gather.16
  248.2 31.1 reduce-scatter.12
  281.9 31.1 reduce-scatter.20
  315.6 57.8 reduce-scatter.8
  375.9 57.8 reduce-scatter.16
  437.2 62.6 reduce-scatter.14
  503.1 61.5 reduce-scatter.22
  568.1 64.4 reduce-scatter.10
  635.9 64.6 reduce-scatter.18
where the time goes:
time: 718 us; the launch traced here: 717 us
  waiting for transfers between devices  465 us (65%)
  blocking collectives  136 us (19%)
  matrix products  83.5 us (12%)
  between operations  14.3 us (2%)
  local copies, waits for them, and re-layouts  11 us (2%)
    reduce_scatter x2, waiting for transfers between devices, reduce_grads(): lax.psum_scatter(qkv_sum.astype(jnp.bfloat16), 'fsdp', scatter_dimension=...  118 us
    reduce_scatter x2, waiting for transfers between devices, reduce_grads(): lax.psum_scatter(qkv_term.astype(jnp.bfloat16), 'rep', scatter_dimension=...  114 us
    all_gather x2, waiting for transfers between devices, fetch(): lax.all_gather(qkv_part, 'fsdp', axis=0, tiled=True)  92.1 us
    reduce_scatter x2, waiting for transfers between devices, reduce_grads(): lax.psum_scatter(out_sum.astype(jnp.bfloat16), 'fsdp', scatter_dimension=...  77.6 us
    all_gather x2, blocking collectives, fetch(): lax.all_gather(out_part, 'fsdp', axis=0, tiled=True)  66.5 us
    reduce_scatter x2, waiting for transfers between devices, reduce_grads(): lax.psum_scatter(out_term.astype(jnp.bfloat16), 'rep', scatter_dimension=...  40.1 us
    psum x1, blocking collectives, per_device(): lax.psum((video_sums[2], audio_sums[2]), ('fsdp', 'rep'))  39.5 us
    all_gather x2, blocking collectives, reduce_grads(): lax.all_gather(qkv_sum.astype(jnp.bfloat16), 'rep', axis=1, tiled=True)  17.7 us
  transfers between devices with their start and end apart: 14, of which 12 were waited for; matrix products, arithmetic and copies ran while one was open for 13% of the time, Pallas kernels for 0%

commit v1 on v0

--- a/solution.py
+++ b/solution.py
@@ -4,6 +4,27 @@
 from jax.sharding import PartitionSpec as P
 
 HEAD = 64
+
+
+def in_order(parts, dim):
+    parts = jnp.moveaxis(parts, 0, dim)
+    dims = parts.shape
+    return parts.reshape(*dims[:dim], dims[dim] * dims[dim + 1], *dims[dim + 2 :])
+
+
+def grow_blocks(x, axis):
+    length, index = (lax.axis_size(axis), lax.axis_index(axis))
+    pieces, bit = (x[None], 1)
+    while bit < length:
+        other = lax.ppermute(pieces, axis, [(i, i ^ bit) for i in range(length)])
+        low = index & bit == 0
+        pieces = jnp.concatenate([jnp.where(low, pieces, other), jnp.where(low, other, pieces)])
+        bit *= 2
+    return pieces
+
+
+def gather_by_bits(shard, axis, dim):
+    return in_order(grow_blocks(shard, axis), dim)
 
 
 def stream(tokens, bottle, gain, w_qkv, w_out, d_tokens, bottle_half):
@@ -76,7 +97,7 @@
     qkv_part = lax.dynamic_slice_in_dim(qkv_shard, place * qkv_cols, qkv_cols, 1)
     out_part = lax.dynamic_slice_in_dim(out_shard, place * out_cols, out_cols, 1)
     qkv_part, out_part = (
-        lax.all_gather(qkv_part, "fsdp", axis=0, tiled=True),
+        gather_by_bits(qkv_part, "fsdp", 0),
         lax.all_gather(out_part, "fsdp", axis=0, tiled=True),
     )
     return (

time: 718 us -> 688 us (0.958)
  waiting for transfers between devices: 465 us -> 417 us
  starting transfers between devices: 0.96 us -> 14.3 us
    ppermute x0 -> x6, waiting for transfers between devices: none -> 93 us  [grow_blocks(): other = lax.ppermute(pieces, axis, [(i, i ^ bit) for i in range(length)])]
    all_gather x2 -> x0, waiting for transfers between devices: 92.1 us -> none  [fetch(): lax.all_gather(qkv_part, 'fsdp', axis=0, tiled=True)]
    reduce_scatter x2, waiting for transfers between devices: 40.1 us -> 13.2 us  [reduce_grads(): lax.psum_scatter(out_term.astype(jnp.bfloat16), 'rep', scatter_dimension=...]
    ppermute x0 -> x6, starting transfers between devices: none -> 13.4 us  [grow_blocks(): other = lax.ppermute(pieces, axis, [(i, i ^ bit) for i in range(length)])]
    all_gather x2, waiting for transfers between devices: 12.2 us -> 0.04 us  [fetch(): lax.all_gather(qkv_part, 'rep', axis=1, tiled=True)]
    all_gather x2, waiting for transfers between devices: 11.1 us -> 0.04 us  [fetch(): lax.all_gather(out_part, 'rep', axis=1, tiled=True)]
  transfers between devices with their start and end apart: 14 -> 18, of which waited for: 12 -> 13; matrix products, arithmetic and copies ran while one was open for 13% -> 14% of each run, Pallas kernels for 0% -> 0%
where the time goes in v1:
time: 688 us; the launch traced here: 687 us
  waiting for transfers between devices  417 us (61%)
  blocking collectives  136 us (20%)
  matrix products  84.5 us (12%)
  between operations  14.7 us (2%)
  starting transfers between devices  14.3 us (2%)
  other arithmetic  10.7 us (2%)
  local copies, waits for them, and re-layouts  9.86 us (1%)
    reduce_scatter x2, waiting for transfers between devices, reduce_grads(): lax.psum_scatter(qkv_sum.astype(jnp.bfloat16), 'fsdp', scatter_dimension=...  118 us
    reduce_scatter x2, waiting for transfers between devices, reduce_grads(): lax.psum_scatter(qkv_term.astype(jnp.bfloat16), 'rep', scatter_dimension=...  114 us
    ppermute x6, waiting for transfers between devices, grow_blocks(): other = lax.ppermute(pieces, axis, [(i, i ^ bit) for i in range(length)])  93 us
    reduce_scatter x2, waiting for transfers between devices, reduce_grads(): lax.psum_scatter(out_sum.astype(jnp.bfloat16), 'fsdp', scatter_dimension=...  77.8 us
    all_gather x2, blocking collectives, fetch(): lax.all_gather(out_part, 'fsdp', axis=0, tiled=True)  67.1 us
    psum x1, blocking collectives, per_device(): lax.psum((video_sums[2], audio_sums[2]), ('fsdp', 'rep'))  39.5 us
    all_gather x2, blocking collectives, reduce_grads(): lax.all_gather(qkv_sum.astype(jnp.bfloat16), 'rep', axis=1, tiled=True)  17.8 us
  transfers between devices with their start and end apart: 18, of which 13 were waited for; matrix products, arithmetic and copies ran while one was open for 14% of the time, Pallas kernels for 0%

profile of v1, /device:TPU:0, one launch (start us, length us, event | category | flops | bytes accessed | tf_op | source)
XLA Modules:
  0.0 687.1 jit_solution(15988013163680896349)
XLA Ops:
  19.1 8.5 %collective-permute-done.1 = bf16[2,128,768]{2,1,0:T(8,128)(2,1)S(1)} collective-permute-done((bf16[2,128,768]{2,1,0:T(8,128)(2,1)S(1)}, bf16[2,128,768]{2,1,0:T(8,128)(2,1)S(1)}, u32[]{:S(2)}, u32[]{:S(2)}) %collective-permute-start.1) | collective-permute-done | bytes 393248 | tf_op jit(solution)/shard_map/ppermute | solution.py:19
  30.3 33.0 %collective-permute-done.2 = bf16[4,128,768]{2,1,0:T(8,128)(2,1)S(1)} collective-permute-done((bf16[4,128,768]{2,1,0:T(8,128)(2,1)S(1)}, bf16[4,128,768]{2,1,0:T(8,128)(2,1)S(1)}, u32[]{:S(2)}, u32[]{:S(2)}) %collective-permute-start.2) | collective-permute-done | bytes 786464 | tf_op jit(solution)/shard_map/ppermute | solution.py:19
  72.3 8.4 %collective-permute-done.4 = bf16[2,128,768]{2,1,0:T(8,128)(2,1)S(1)} collective-permute-done((bf16[2,128,768]{2,1,0:T(8,128)(2,1)S(1)}, bf16[2,128,768]{2,1,0:T(8,128)(2,1)S(1)}, u32[]{:S(2)}, u32[]{:S(2)}) %collective-permute-start.4) | collective-permute-done | bytes 393248 | tf_op jit(solution)/shard_map/ppermute | solution.py:19
  84.3 33.2 %collective-permute-done.5 = bf16[4,128,768]{2,1,0:T(8,128)(2,1)S(1)} collective-permute-done((bf16[4,128,768]{2,1,0:T(8,128)(2,1)S(1)}, bf16[4,128,768]{2,1,0:T(8,128)(2,1)S(1)}, u32[]{:S(2)}, u32[]{:S(2)}) %collective-permute-start.5) | collective-permute-done | bytes 786464 | tf_op jit(solution)/shard_map/ppermute | solution.py:19
  119.1 33.9 %all_gather.31 = bf16[1024,256]{1,0:T(8,128)(2,1)} all-gather(bf16[128,256]{1,0:T(8,128)(2,1)S(1)} %constant_dynamic-slice_fusion.1), channel_id=1, replica_groups=mesh['fsdp'=8,'rep'=4] {'fsdp'}, dimensions={0}, use_global_device_ids=true | all-gather | bytes 589824 | tf_op jit(solution)/shard_map/all_gather | solution.py:101
  154.0 33.2 %all_gather.34 = bf16[1024,256]{1,0:T(8,128)(2,1)} all-gather(bf16[128,256]{1,0:T(8,128)(2,1)S(1)} %constant_dynamic-slice_fusion), channel_id=1, replica_groups=mesh['fsdp'=8,'rep'=4] {'fsdp'}, dimensions={0}, use_global_device_ids=true | all-gather | bytes 589824 | tf_op jit(solution)/shard_map/all_gather | solution.py:101
  221.9 8.2 %fusion.40 = bf16[16,64,204]{2,1,0:T(8,128)(2,1)} fusion(bf16[204,16,64]{0,2,1:T(8,128)(2,1)} %bitcast.107, f32[16,204,204]{1,2,0:T(8,128)} %fusion.113, f32[16,204,204]{1,2,0:T(8,128)} %get-tuple-element.106, f32[16,204]{1,0:T(8,128)S(1)} %get-tuple-element.105), kind=kOutput, calls=%fused_computation.39 | convolution fusion | flops 90102920 | bytes 6175488 | tf_op jit(solution)/shard_map/while/body/eval_jaxpr/hst,shd->thd/dot_general | solution.py:63
  230.0 7.2 %fusion.37 = bf16[16,64,204]{2,1,0:T(8,128)(2,1)} fusion(bf16[204,16,64]{0,2,1:T(8,128)(2,1)S(1)} %bitcast.109, f32[16,204,204]{1,2,0:T(8,128)} %fusion.113, f32[16,204,204]{1,2,0:T(8,128)} %get-tuple-element.106, f32[16,204]{1,0:T(8,128)S(1)} %get-tuple-element.105), kind=kOutput, calls=%fused_computation.38 | convolution fusion | flops 90102920 | bytes 6175488 | tf_op jit(solution)/shard_map/while/body/eval_jaxpr/hst,thd->shd/dot_general | solution.py:62
  250.1 5.3 fusion.34
  255.4 5.3 fusion.31
  269.3 13.2 %reduce-scatter.21.cloned.1.call-done = bf16[1024,256]{1,0:T(8,128)(2,1)} async-done(((bf16[1024,1024]{1,0:T(8,128)(2,1)}), bf16[1024,256]{1,0:T(8,128)(2,1)}) %reduce-scatter.21.cloned.1.call-update) | async-done | bytes 524304 | tf_op jit(solution)/shard_map/reduce_scatter | solution.py:114
  282.6 60.4 %reduce-scatter.9.cloned.1.call-done = bf16[1024,768]{1,0:T(8,128)(2,1)} async-done(((bf16[1024,3072]{1,0:T(8,128)(2,1)}), bf16[1024,768]{1,0:T(8,128)(2,1)}) %reduce-scatter.9.cloned.1.call-update) | async-done | bytes 1572880 | tf_op jit(solution)/shard_map/reduce_scatter | solution.py:111
  343.3 5.5 fusion.56
  349.8 53.6 %reduce-scatter.17.cloned.1.call-done = bf16[1024,768]{1,0:T(8,128)(2,1)} async-done(((bf16[1024,3072]{1,0:T(8,128)(2,1)}), bf16[1024,768]{1,0:T(8,128)(2,1)}) %reduce-scatter.17.cloned.1.call-update) | async-done | bytes 1572880 | tf_op jit(solution)/shard_map/reduce_scatter | solution.py:111
  403.4 5.5 fusion.73
  409.9 39.5 %all-reduce = (f32[1024]{0:T(1024)S(1)}, f32[1024]{0:T(1024)S(1)}) all-reduce(f32[1024]{0:T(1024)S(1)} %get-tuple-element.57, f32[1024]{0:T(1024)S(1)} %get-tuple-element.59), channel_id=1, replica_groups=mesh['fsdp'=8,'rep'=4] {'fsdp','rep'}, use_global_device_ids=true, to_apply=%region_19.20 | all-reduce | flops 2048 | bytes 16384 | tf_op jit(solution)/shard_map/psum | solution.py:162
  450.6 18.8 %reduce-scatter.15.cloned.1.call-done = bf16[128,256]{1,0:T(8,128)(2,1)} async-done(((bf16[1024,256]{1,0:T(8,128)(2,1)}), bf16[128,256]{1,0:T(8,128)(2,1)}) %reduce-scatter.15.cloned.1.call-update) | async-done | bytes 65552 | tf_op jit(solution)/shard_map/reduce_scatter | solution.py:122
  469.5 6.0 all_gather.37
  475.4 59.0 %reduce-scatter.23.cloned.1.call-done = bf16[128,256]{1,0:T(8,128)(2,1)} async-done(((bf16[1024,256]{1,0:T(8,128)(2,1)}), bf16[128,256]{1,0:T(8,128)(2,1)}) %reduce-scatter.23.cloned.1.call-update) | async-done | bytes 65552 | tf_op jit(solution)/shard_map/reduce_scatter | solution.py:122
  534.4 6.0 all_gather.39
  542.1 60.2 %reduce-scatter.11.cloned.1.call-done = bf16[128,768]{1,0:T(8,128)(2,1)} async-done(((bf16[1024,768]{1,0:T(8,128)(2,1)}), bf16[128,768]{1,0:T(8,128)(2,1)}) %reduce-scatter.11.cloned.1.call-update) | async-done | bytes 196624 | tf_op jit(solution)/shard_map/reduce_scatter | solution.py:119
  602.3 8.9 %all_gather.36 = bf16[128,3072]{1,0:T(8,128)(2,1)S(1)} all-gather(bf16[128,768]{1,0:T(8,128)(2,1)} %reduce-scatter.11.cloned.1.call-done), channel_id=1, replica_groups=mesh['fsdp'=8,'rep'=4] {'rep'}, dimensions={1}, use_global_device_ids=true | all-gather | bytes 983040 | tf_op jit(solution)/shard_map/all_gather | solution.py:127
  612.5 57.5 %reduce-scatter.19.cloned.1.call-done = bf16[128,768]{1,0:T(8,128)(2,1)} async-done(((bf16[1024,768]{1,0:T(8,128)(2,1)}), bf16[128,768]{1,0:T(8,128)(2,1)}) %reduce-scatter.19.cloned.1.call-update) | async-done | bytes 196624 | tf_op jit(solution)/shard_map/reduce_scatter | solution.py:119
  670.0 8.9 %all_gather.38 = bf16[128,3072]{1,0:T(8,128)(2,1)S(1)} all-gather(bf16[128,768]{1,0:T(8,128)(2,1)} %reduce-scatter.19.cloned.1.call-done), channel_id=1, replica_groups=mesh['fsdp'=8,'rep'=4] {'rep'}, dimensions={1}, use_global_device_ids=true | all-gather | bytes 983040 | tf_op jit(solution)/shard_map/all_gather | solution.py:127
  (150 shorter events, 93.2 us)
Async XLA Ops:
  7.2 111.9 %copy-start = (bf16[128,1024]{1,0:T(8,128)(2,1)S(1)}, bf16[128,1024]{1,0:T(8,128)(2,1)}, u32[]{:S(2)}) copy-start(bf16[128,1024]{1,0:T(8,128)(2,1)} %param.18) | copy-start | bytes 786436
  7.2 180.4 %all-gather.5.cloned.1.call-start = ((), (), s32[]{:S(2)}) async-start(), calls=%async_computation.8 | async-start | bytes 7864320 | tf_op jit(solution)/shard_map/all_gather | solution.py:104
  8.2 7.9 %collective-permute-start = (bf16[1,128,768]{2,1,0:T(8,128)(2,1)S(1)}, bf16[1,128,768]{2,1,0:T(8,128)(2,1)S(1)}, u32[]{:S(2)}, u32[]{:S(2)}) collective-permute-start(bf16[1,128,768]{2,1,0:T(8,128)(2,1)S(1)} %dynamic-slice_bitcast_fusion.1), channel_id=1, source_target_pairs={{0,4},{4,0},{8,12},{12,8},{16,20},{20,16},{24,28},{28,24},{1,5},{5... | collective-permute-start | bytes 589832 | tf_op jit(solution)/shard_map/ppermute | solution.py:19
  17.2 10.3 %collective-permute-start.1 = (bf16[2,128,768]{2,1,0:T(8,128)(2,1)S(1)}, bf16[2,128,768]{2,1,0:T(8,128)(2,1)S(1)}, u32[]{:S(2)}, u32[]{:S(2)}) collective-permute-start(bf16[2,128,768]{2,1,0:T(8,128)(2,1)S(1)} %pad_maximum_fusion.13), channel_id=1, source_target_pairs={{0,8},{4,12},{8,0},{12,4},{16,24},{20,28},{24,16},{28,20},{1,9},{5... | collective-permute-start | bytes 1179656 | tf_op jit(solution)/shard_map/ppermute | solution.py:19
  27.7 35.7 %collective-permute-start.2 = (bf16[4,128,768]{2,1,0:T(8,128)(2,1)S(1)}, bf16[4,128,768]{2,1,0:T(8,128)(2,1)S(1)}, u32[]{:S(2)}, u32[]{:S(2)}) collective-permute-start(bf16[4,128,768]{2,1,0:T(8,128)(2,1)S(1)} %pad_maximum_fusion.5), channel_id=1, source_target_pairs={{0,16},{4,20},{8,24},{12,28},{16,0},{20,4},{24,8},{28,12},{1,17},{... | collective-permute-start | bytes 2359304 | tf_op jit(solution)/shard_map/ppermute | solution.py:19
  64.8 135.9 %all-gather.9.cloned.1.call-start = ((), (), s32[]{:S(2)}) async-start(), calls=%async_computation.10 | async-start | bytes 7864320 | tf_op jit(solution)/shard_map/all_gather | solution.py:104
  64.9 6.2 collective-permute-start.3
  71.2 9.6 %collective-permute-start.4 = (bf16[2,128,768]{2,1,0:T(8,128)(2,1)S(1)}, bf16[2,128,768]{2,1,0:T(8,128)(2,1)S(1)}, u32[]{:S(2)}, u32[]{:S(2)}) collective-permute-start(bf16[2,128,768]{2,1,0:T(8,128)(2,1)S(1)} %pad_maximum_fusion.14), channel_id=1, source_target_pairs={{0,8},{4,12},{8,0},{12,4},{16,24},{20,28},{24,16},{28,20},{1,9},{5... | collective-permute-start | bytes 1179656 | tf_op jit(solution)/shard_map/ppermute | solution.py:19
  80.9 36.7 %collective-permute-start.5 = (bf16[4,128,768]{2,1,0:T(8,128)(2,1)S(1)}, bf16[4,128,768]{2,1,0:T(8,128)(2,1)S(1)}, u32[]{:S(2)}, u32[]{:S(2)}) collective-permute-start(bf16[4,128,768]{2,1,0:T(8,128)(2,1)S(1)} %pad_maximum_fusion.6), channel_id=1, source_target_pairs={{0,16},{4,20},{8,24},{12,28},{16,0},{20,4},{24,8},{28,12},{1,17},{... | collective-permute-start | bytes 2359304 | tf_op jit(solution)/shard_map/ppermute | solution.py:19
  119.0 68.5 %copy-start.11 = (bf16[1,196,1024]{2,1,0:T(8,128)(2,1)S(1)}, bf16[1,196,1024]{2,1,0:T(8,128)(2,1)}, u32[]{:S(2)}) copy-start(bf16[1,196,1024]{2,1,0:T(8,128)(2,1)} %param.21) | copy-start | bytes 1204228
  119.0 68.6 %copy-start.16 = (f32[1024]{0:T(1024)S(1)}, f32[1024]{0:T(1024)}, u32[]{:S(2)}) copy-start(f32[1024]{0:T(1024)} %param.15) | copy-start | bytes 12292
  119.0 96.0 %all-gather.7.cloned.1.call-start = ((), (), s32[]{:S(2)}) async-start(), calls=%async_computation.9 | async-start | bytes 2621440 | tf_op jit(solution)/shard_map/all_gather | solution.py:105
  153.1 92.4 %all-gather.11.cloned.1.call-start = ((), (), s32[]{:S(2)}) async-start(), calls=%async_computation.11 | async-start | bytes 2621440 | tf_op jit(solution)/shard_map/all_gather | solution.py:105
  187.2 81.3 %reduce-scatter.13.cloned.1.call-start = ((), (), s32[]{:S(2)}) async-start(), calls=%async_computation.14 | async-start | bytes 2621440 | tf_op jit(solution)/shard_map/reduce_scatter | solution.py:114
  200.4 82.1 %reduce-scatter.21.cloned.1.call-start = ((), (), s32[]{:S(2)}) async-start(), calls=%async_computation.18 | async-start | bytes 2621440 | tf_op jit(solution)/shard_map/reduce_scatter | solution.py:114
  214.8 128.1 %reduce-scatter.9.cloned.1.call-start = ((), (), s32[]{:S(2)}) async-start(), calls=%async_computation.12 | async-start | bytes 7864320 | tf_op jit(solution)/shard_map/reduce_scatter | solution.py:111
  245.4 158.0 %reduce-scatter.17.cloned.1.call-start = ((), (), s32[]{:S(2)}) async-start(), calls=%async_computation.16 | async-start | bytes 7864320 | tf_op jit(solution)/shard_map/reduce_scatter | solution.py:111
  268.5 74.8 %copy-start.4 = (bf16[1,196,1024]{2,1,0:T(8,128)(2,1)S(1)}, bf16[1,196,1024]{2,1,0:T(8,128)(2,1)}, u32[]{:S(2)}) copy-start(bf16[1,196,1024]{2,1,0:T(8,128)(2,1)} %param.12) | copy-start | bytes 1204228
  268.5 74.8 %copy-start.19 = (bf16[16,64,204]{2,1,0:T(8,128)(2,1)S(1)}, bf16[16,64,204]{2,1,0:T(8,128)(2,1)}, u32[]{:S(2)}) copy-start(bf16[16,64,204]{2,1,0:T(8,128)(2,1)} %fusion.40) | copy-start | bytes 1253380
  268.5 200.9 %reduce-scatter.15.cloned.1.call-start = ((), (), s32[]{:S(2)}) async-start(), calls=%async_computation.15 | async-start | bytes 589824 | tf_op jit(solution)/shard_map/reduce_scatter | solution.py:122
  269.2 265.2 %reduce-scatter.23.cloned.1.call-start = ((), (), s32[]{:S(2)}) async-start(), calls=%async_computation.19 | async-start | bytes 589824 | tf_op jit(solution)/shard_map/reduce_scatter | solution.py:122
  282.5 319.8 %reduce-scatter.11.cloned.1.call-start = ((), (), s32[]{:S(2)}) async-start(), calls=%async_computation.13 | async-start | bytes 1769472 | tf_op jit(solution)/shard_map/reduce_scatter | solution.py:119
  343.0 327.0 %reduce-scatter.19.cloned.1.call-start = ((), (), s32[]{:S(2)}) async-start(), calls=%async_computation.17 | async-start | bytes 1769472 | tf_op jit(solution)/shard_map/reduce_scatter | solution.py:119
  611.2 69.0 %copy-start.1 = (bf16[128,1024]{1,0:T(8,128)(2,1)S(1)}, bf16[128,1024]{1,0:T(8,128)(2,1)}, u32[]{:S(2)}) copy-start(bf16[128,1024]{1,0:T(8,128)(2,1)} %param.18) | copy-start | bytes 786436
  (20 other events, 306.1 us)
Sparse Core Ops, SparseCore 0:
  64.9 47.1 all-gather.4
  119.1 47.5 all-gather.8
  168.3 22.8 all-gather.6
  192.5 22.8 all-gather.10
  217.7 31.1 reduce-scatter.12
  251.4 31.0 reduce-scatter.20
  285.0 57.8 reduce-scatter.8
  345.5 57.8 reduce-scatter.16
  406.8 62.6 reduce-scatter.14
  472.6 61.7 reduce-scatter.22
  537.8 64.4 reduce-scatter.10
  605.6 64.3 reduce-scatter.18
